TPU v7x, 512 devices: a whole 4x4x16 slice. The times are simulated.
512 devices in a mesh: seq: 4 (over y_lo, core), head: 8 (over x, y_hi), dp: 16 (over z).
Axes of the slice: x: 4, y: 4 (y_hi: 2, y_lo: 2; y = y_hi * 2 + y_lo), z: 16, core: 2. Of those that a mesh axis runs over, the one named last changes fastest.
Arguments:
- queries: bfloat16 [16, 2048, 4096], P('dp', 'seq', 'head'), may hold values from -2 to 2
- keys: bfloat16 [16, 2048, 4096], P('dp', 'seq', 'head'), may hold values from -2 to 2
- values: bfloat16 [16, 2048, 4096], P('dp', 'seq', 'head'), may hold values from -6 to 6
- out_proj: bfloat16 [4096, 1024], P('head', 'dp'), may hold values from -0.09375 to 0.09375
- depth_proj: bfloat16 [1024, 1024], P(None, ('head', 'dp')), may hold values from -0.1875 to 0.1875
- code_table: bfloat16 [2, 1024, 1024], P(None, ('head', 'dp')), may hold values from -6 to 6
- code_ids: int32 [16, 2048, 2], P('dp', ('seq', 'head')), may hold values from 0 to 1023
- depth_cotangent: bfloat16 [16, 2048, 2, 1024], P('dp', ('seq', 'head')), may hold values from -6 to 6
Outputs:
- grad_queries: bfloat16 [16, 2048, 4096], P('dp', 'seq', 'head')
- grad_keys: bfloat16 [16, 2048, 4096], P('dp', 'seq', 'head')
- grad_values: bfloat16 [16, 2048, 4096], P('dp', 'seq', 'head')
- grad_out_proj: float32 [4096, 1024], P('head', 'dp')
All inputs are finite; a program needn't handle non-finite values.
Results may differ from a plain program's by a relative error of at most 0.024.
Values may be sent and summed in bfloat16 or wider, within the bound.
A program may use at most 64 MiB of HBM per device.

v0:
```python
import jax
import jax.numpy as jnp
from jax import lax
from jax.sharding import PartitionSpec as P

DH = 128


def from_behind(block, axis, distance):
    devices = range(lax.axis_size(axis))
    route = [(i - distance, i) for i in devices if i - distance in devices]
    return lax.ppermute(block, axis, route)


def causal_mask(size):
    places = jnp.arange(size, dtype=jnp.int32)
    return (places[:, None] >= places[None, :]).astype(jnp.float32)


def depth_forward(carried, code_tab, proj_mat, code_rows):
    vocab_idx = jnp.arange(code_tab.shape[1], dtype=jnp.int32)
    level_outs = []
    for level_idx in range(code_tab.shape[0]):
        onehot = (code_rows[:, level_idx][:, None] == vocab_idx[None, :]).astype(jnp.bfloat16)
        embedded = jnp.dot(onehot, code_tab[level_idx], preferred_element_type=jnp.float32)
        summed = carried + embedded
        normed = (
            summed * lax.rsqrt(jnp.mean(summed * summed, axis=-1, keepdims=True) + 1e-05)
        ).astype(jnp.bfloat16)
        projected = jnp.dot(normed, proj_mat, preferred_element_type=jnp.float32)
        level_outs.append(projected)
        carried = summed + jax.nn.silu(projected)
    return jnp.stack(level_outs, axis=1)


def on_device(queries, keys, values, out_proj, depth_proj, code_table, code_ids, depth_cotangent):
    group_len = queries.shape[1]
    width_dev = queries.shape[2]
    heads_here = width_dev // DH
    att_scale = float(group_len * lax.axis_size("seq")) ** (-0.5)
    query_rows = queries[0].reshape(group_len, heads_here, DH)
    key_rows = keys[0].reshape(group_len, heads_here, DH)
    value_rows = values[0].reshape(group_len, heads_here, DH)
    causal = causal_mask(group_len)
    state_zero = jnp.zeros((heads_here, DH, DH), jnp.float32)
    state_local = jnp.einsum(
        "thd,the->hde", key_rows, value_rows, preferred_element_type=jnp.float32
    )
    state_acc = state_zero
    moving = state_local
    for hop_idx in range(lax.axis_size("seq") - 1):
        moving = from_behind(moving.astype(jnp.bfloat16), "seq", 1).astype(moving.dtype)
        state_acc = state_acc + moving
    state_in = state_acc.astype(jnp.bfloat16)
    scores = (
        jnp.einsum("thd,shd->hts", query_rows, key_rows, preferred_element_type=jnp.float32)
        * causal
    ).astype(jnp.bfloat16)
    attended = (
        att_scale
        * (
            jnp.einsum("hts,she->the", scores, value_rows, preferred_element_type=jnp.float32)
            + jnp.einsum("thd,hde->the", query_rows, state_in, preferred_element_type=jnp.float32)
        )
    ).astype(jnp.bfloat16)
    attended_flat = attended.reshape(group_len, width_dev)
    proj_full = lax.all_gather(out_proj, "dp", axis=1, tiled=True)
    mixed = lax.psum_scatter(
        jnp.dot(attended_flat, proj_full, preferred_element_type=jnp.float32).astype(jnp.bfloat16),
        "head",
        scatter_dimension=0,
        tiled=True,
    ).astype(jnp.float32)
    proj_mat, code_tab = (
        lax.all_gather(depth_proj, ("head", "dp"), axis=1, tiled=True),
        lax.all_gather(code_table, ("head", "dp"), axis=1, tiled=True),
    )
    code_rows = code_ids[0]
    cotangent = depth_cotangent[0].astype(jnp.float32)
    _, pullback = jax.vjp(
        lambda inputs: depth_forward(inputs, code_tab, proj_mat, code_rows), mixed
    )
    grad_mixed = pullback(cotangent)[0].astype(jnp.bfloat16)
    grad_block = lax.all_gather(grad_mixed, "head", axis=0, tiled=True)
    grad_att = lax.dot_general(
        grad_block, proj_full, (((1,), (1,)), ((), ())), preferred_element_type=jnp.float32
    )
    grad_rows = grad_att.astype(jnp.bfloat16).reshape(group_len, heads_here, DH)
    weight_term = lax.dot_general(
        attended_flat, grad_block, (((0,), (0,)), ((), ())), preferred_element_type=jnp.float32
    )
    weight_part = lax.psum_scatter(
        weight_term.astype(jnp.bfloat16), "dp", scatter_dimension=1, tiled=True
    )
    grad_out_proj = lax.psum(weight_part, "seq").astype(jnp.float32)
    back_local = jnp.einsum(
        "thd,the->hde", query_rows, grad_rows, preferred_element_type=jnp.float32
    )
    back_acc = state_zero
    moving_back = back_local
    for hop_idx in range(lax.axis_size("seq") - 1):
        moving_back = from_behind(moving_back.astype(jnp.bfloat16), "seq", -1).astype(
            moving_back.dtype
        )
        back_acc = back_acc + moving_back
    back_state = back_acc.astype(jnp.bfloat16)
    grad_scores = (
        jnp.einsum("the,she->hts", grad_rows, value_rows, preferred_element_type=jnp.float32)
        * causal
    ).astype(jnp.bfloat16)
    grad_query = att_scale * (
        jnp.einsum("hts,shd->thd", grad_scores, key_rows, preferred_element_type=jnp.float32)
        + jnp.einsum("the,hde->thd", grad_rows, state_in, preferred_element_type=jnp.float32)
    )
    grad_key = att_scale * (
        jnp.einsum("hts,thd->shd", grad_scores, query_rows, preferred_element_type=jnp.float32)
        + jnp.einsum("she,hde->shd", value_rows, back_state, preferred_element_type=jnp.float32)
    )
    grad_value = att_scale * (
        jnp.einsum("hts,the->she", scores, grad_rows, preferred_element_type=jnp.float32)
        + jnp.einsum("shd,hde->she", key_rows, back_state, preferred_element_type=jnp.float32)
    )
    out_shape = (1, group_len, width_dev)
    return (
        grad_query.reshape(out_shape).astype(jnp.bfloat16),
        grad_key.reshape(out_shape).astype(jnp.bfloat16),
        grad_value.reshape(out_shape).astype(jnp.bfloat16),
        grad_out_proj,
    )


def solution(mesh):
    in_specs = (
        P("dp", "seq", "head"),
        P("dp", "seq", "head"),
        P("dp", "seq", "head"),
        P("head", "dp"),
        P(None, ("head", "dp")),
        P(None, ("head", "dp"), None),
        P("dp", ("seq", "head"), None),
        P("dp", ("seq", "head"), None, None),
    )
    out_specs = (
        P("dp", "seq", "head"),
        P("dp", "seq", "head"),
        P("dp", "seq", "head"),
        P("head", "dp"),
    )
    return jax.shard_map(
        on_device, mesh=mesh, in_specs=in_specs, out_specs=out_specs, check_vma=False
    )
```

profile of v0, /device:TPU:1, one launch (start us, length us, event | category | flops | bytes accessed | tf_op | source)
XLA Modules:
  0.0 812.8 jit_solution(11603275540361019960)
XLA Ops:
  7.2 0.0 all-gather.7.cloned.1.call-start
  7.2 0.7 all-gather.7.cloned.1.call-update
  7.9 0.0 all-gather.5.cloned.1.call-start
  8.0 0.7 all-gather.5.cloned.1.call-update
  8.7 0.0 reduce-scatter.3.cloned.1.call-start
  8.7 1.2 reshape_squeeze.10
  9.9 0.3 copy.16
  10.3 0.1 reshape_squeeze.11
  10.4 0.3 convolution_convert_fusion.5
  10.7 4.6 collective-permute-start
  15.3 0.9 reshape_squeeze.9
  16.3 0.1 fusion.18
  16.4 3.3 collective-permute-done
  19.7 1.9 collective-permute-start.1
  21.6 2.0 multiply_convert_fusion.1
  23.6 4.2 collective-permute-start.2
  27.9 0.8 convolution_bitcast_fusion.2
  28.7 1.1 collective-permute-done.2
  29.8 1.2 fusion.9
  31.0 44.8 %all-gather.7.cloned.1.call-done = bf16[512,1024]{0,1:T(8,128)(2,1)} async-done(((bf16[512,64]{0,1:T(8,128)(2,1)}), bf16[512,1024]{0,1:T(8,128)(2,1)}) %all-gather.7.cloned.1.call-update) | async-done | bytes 1048592 | tf_op jit(solution)/shard_map/all_gather | solution.py:67
  75.7 3.2 convolution_convert_fusion.1
  79.0 0.0 reduce-scatter.3.cloned.1.call-update
  79.0 0.0 all-gather.9.cloned.1.call-start
  79.0 0.5 all-gather.9.cloned.1.call-update
  79.6 0.0 all-gather.11.cloned.1.call-start
  79.6 1.7 copy.57
  81.3 210.8 %all-gather.5.cloned.1.call-done = bf16[1024,1024]{0,1:T(8,128)(2,1)} async-done(((bf16[1024,8]{0,1:T(8,128)(2,1)}), bf16[1024,1024]{0,1:T(8,128)(2,1)}) %all-gather.5.cloned.1.call-update) | async-done | bytes 2097168 | tf_op jit(solution)/shard_map/all_gather | solution.py:75
  292.2 2.1 fusion.16
  294.3 92.4 %reduce-scatter.3.cloned.1.call-done = bf16[64,1024]{1,0:T(8,128)(2,1)} async-done(((bf16[512,1024]{1,0:T(8,128)(2,1)}), bf16[64,1024]{1,0:T(8,128)(2,1)}) %reduce-scatter.3.cloned.1.call-update) | async-done | bytes 131088 | tf_op jit(solution)/shard_map/reduce_scatter | solution.py:68
  386.7 218.7 %all-gather.9.cloned.1.call-done = bf16[2,1024,1024]{2,1,0:T(8,128)(2,1)} async-done(((bf16[2,8,1024]{2,1,0:T(8,128)(2,1)}), bf16[2,1024,1024]{2,1,0:T(8,128)(2,1)}) %all-gather.9.cloned.1.call-update) | async-done | bytes 4194320 | tf_op jit(solution)/shard_map/all_gather | solution.py:76
  605.5 2.4 multiply_reduce_fusion.3
  607.9 0.8 fusion.37
  608.6 2.3 multiply_reduce_fusion.2
  611.0 0.7 multiply_reduce_fusion
  611.7 0.8 fusion.33
  612.5 0.0 all-gather.11.cloned.1.call-update
  612.6 0.0 reduce-scatter.5.cloned.1.call-start
  612.6 64.7 %all-gather.11.cloned.1.call-done = bf16[512,1024]{1,0:T(8,128)(2,1)} async-done(((bf16[64,1024]{1,0:T(8,128)(2,1)}), bf16[512,1024]{1,0:T(8,128)(2,1)}) %all-gather.11.cloned.1.call-update) | async-done | bytes 1048592 | tf_op jit(solution)/shard_map/all_gather | solution.py:84
  677.3 3.1 convolution_convert_fusion
  680.4 0.0 reduce-scatter.5.cloned.1.call-update
  680.4 0.0 all-reduce.2.cloned.1.call-start
  680.5 0.0 copy-start.6
  680.5 2.4 convolution_convert_fusion.2
  682.9 0.3 fusion.17
  683.2 4.3 collective-permute-start.3
  687.5 1.4 fusion.45
  688.9 0.8 multiply_convert_fusion
  689.7 0.5 convolution_bitcast_fusion
  690.2 0.1 collective-permute-done.3
  690.3 1.9 collective-permute-start.4
  692.3 0.8 convolution_bitcast_fusion.1
  693.1 3.6 collective-permute-done.4
  696.7 1.9 collective-permute-start.5
  698.6 1.1 fusion.10
  699.7 2.1 copy.29
  701.8 1.5 collective-permute-done.5
  703.3 2.1 fusion.12
  705.4 36.8 %reduce-scatter.5.cloned.1.call-done = bf16[512,64]{0,1:T(8,128)(2,1)} async-done(((bf16[512,1024]{0,1:T(8,128)(2,1)}), bf16[512,64]{0,1:T(8,128)(2,1)}) %reduce-scatter.5.cloned.1.call-update) | async-done | bytes 65552 | tf_op jit(solution)/shard_map/reduce_scatter | solution.py:92
  742.2 0.0 all-reduce.2.cloned.1.call-update
  742.3 1.3 fusion.11
  743.6 1.0 copy.31
  744.6 1.0 copy.30
  745.6 58.9 %all-reduce.2.cloned.1.call-done = bf16[512,64]{0,1:T(8,128)(2,1)} async-done(((bf16[512,64]{0,1:T(8,128)(2,1)}), bf16[512,64]{0,1:T(8,128)(2,1)}) %all-reduce.2.cloned.1.call-update) | async-done | bytes 65552 | tf_op jit(solution)/shard_map/psum | solution.py:95
  804.5 1.5 convert_element_type.168
  (50 shorter events, 0.1 us)
Async XLA Ops:
  7.2 3.1 copy-start.20
  7.2 68.6 %all-gather.7.cloned.1.call-start = ((), (), s32[]{:S(2)}) async-start(), calls=%async_computation.3 | async-start | bytes 1114112 | tf_op jit(solution)/shard_map/all_gather | solution.py:67
  7.9 284.3 %all-gather.5.cloned.1.call-start = ((), (), s32[]{:S(2)}) async-start(), calls=%async_computation.2 | async-start | bytes 2113536 | tf_op jit(solution)/shard_map/all_gather | solution.py:75
  8.7 6.7 copy-start.21
  8.7 378.1 %reduce-scatter.3.cloned.1.call-start = ((), (), s32[]{:S(2)}) async-start(), calls=%async_computation.4 | async-start | bytes 1179648 | tf_op jit(solution)/shard_map/reduce_scatter | solution.py:68
  9.9 5.4 copy-start.7
  10.3 5.0 copy-start.10
  10.4 9.3 %copy-start.1 = (bf16[512,4,128]{2,1,0:T(4,128)(2,1)}, bf16[512,4,128]{2,1,0:T(4,128)(2,1)S(1)}, u32[]{:S(2)}) copy-start(bf16[512,4,128]{2,1,0:T(4,128)(2,1)S(1)} %reshape_squeeze.11) | copy-start | bytes 1572868
  10.7 9.0 %collective-permute-start = (bf16[4,128,128]{2,1,0:T(8,128)(2,1)S(1)}, bf16[4,128,128]{2,1,0:T(8,128)(2,1)S(1)}, u32[]{:S(2)}, u32[]{:S(2)}) collective-permute-start(bf16[4,128,128]{2,1,0:T(8,128)(2,1)S(1)} %convolution_convert_fusion.5), channel_id=1, source_target_pairs={{0,128},{128,256},{256,384},{1,129},{129,257},{257,385},{2,130},{1... | collective-permute-start | bytes 393224 | tf_op jit(solution)/shard_map/ppermute | solution.py:12
  19.7 3.9 collective-permute-start.1
  21.6 6.3 copy-start.2
  23.6 6.2 copy-start.5
  23.6 7.4 copy-start.14
  23.6 6.2 collective-permute-start.2
  29.8 49.2 %copy-start.16 = (bf16[4,128,128]{2,1,0:T(8,128)(2,1)}, bf16[4,128,128]{2,1,0:T(8,128)(2,1)S(1)}, u32[]{:S(2)}) copy-start(bf16[4,128,128]{2,1,0:T(8,128)(2,1)S(1)} %collective-permute-done.2) | copy-start | bytes 393220
  75.7 5.6 copy-start.22
  79.0 526.5 %all-gather.9.cloned.1.call-start = ((), (), s32[]{:S(2)}) async-start(), calls=%async_computation.5 | async-start | bytes 4227072 | tf_op jit(solution)/shard_map/all_gather | solution.py:76
  79.6 597.7 %all-gather.11.cloned.1.call-start = ((), (), s32[]{:S(2)}) async-start(), calls=%async_computation.6 | async-start | bytes 1179648 | tf_op jit(solution)/shard_map/all_gather | solution.py:84
  605.5 2.4 copy-start
  608.6 2.3 copy-start.13
  612.6 129.7 %reduce-scatter.5.cloned.1.call-start = ((), (), s32[]{:S(2)}) async-start(), calls=%async_computation.7 | async-start | bytes 1114112 | tf_op jit(solution)/shard_map/reduce_scatter | solution.py:92
  680.4 124.0 %all-reduce.2.cloned.1.call-start = ((), (), s32[]{:S(2)}) async-start(), calls=%async_computation.8 | async-start | bytes 131072 | tf_op jit(solution)/shard_map/psum | solution.py:95
  680.5 2.4 copy-start.6
  683.2 5.7 copy-start.3
  683.2 7.1 collective-permute-start.3
  689.7 2.6 copy-start.11
  690.2 8.4 %copy-start.15 = (bf16[4,128,128]{2,1,0:T(8,128)(2,1)S(1)}, bf16[4,128,128]{2,1,0:T(8,128)(2,1)}, u32[]{:S(2)}) copy-start(bf16[4,128,128]{2,1,0:T(8,128)(2,1)} %copy-done.14) | copy-start | bytes 393220
  690.2 8.4 %copy-start.17 = (bf16[4,128,128]{2,1,0:T(8,128)(2,1)S(1)}, bf16[4,128,128]{2,1,0:T(8,128)(2,1)}, u32[]{:S(2)}) copy-start(bf16[4,128,128]{2,1,0:T(8,128)(2,1)} %copy-done.16) | copy-start | bytes 393220
  690.3 9.4 %copy-start.18 = (bf16[4,128,128]{1,2,0:T(8,128)(2,1)}, bf16[4,128,128]{1,2,0:T(8,128)(2,1)S(1)}, u32[]{:S(2)}) copy-start(bf16[4,128,128]{1,2,0:T(8,128)(2,1)S(1)} %collective-permute-done.3) | copy-start | bytes 393220
  690.3 6.4 collective-permute-start.4
  693.1 10.2 %copy-start.8 = (bf16[512,4,128]{2,1,0:T(4,128)(2,1)S(1)}, bf16[512,4,128]{2,1,0:T(4,128)(2,1)}, u32[]{:S(2)}) copy-start(bf16[512,4,128]{2,1,0:T(4,128)(2,1)} %copy-done.7) | copy-start | bytes 1572868
  693.1 10.2 %copy-start.9 = (f32[4,128,512]{2,1,0:T(8,128)S(1)}, f32[4,128,512]{2,1,0:T(8,128)}, u32[]{:S(2)}) copy-start(f32[4,128,512]{2,1,0:T(8,128)} %fusion.45) | copy-start | bytes 3145732
  696.7 6.6 collective-permute-start.5
  699.7 42.5 %copy-start.4 = (bf16[512,4,128]{2,1,0:T(4,128)(2,1)S(1)}, bf16[512,4,128]{2,1,0:T(4,128)(2,1)}, u32[]{:S(2)}) copy-start(bf16[512,4,128]{2,1,0:T(4,128)(2,1)} %copy-done.1) | copy-start | bytes 1572868
  699.7 42.5 %copy-start.19 = (bf16[4,128,128]{1,2,0:T(8,128)(2,1)S(1)}, bf16[4,128,128]{1,2,0:T(8,128)(2,1)}, u32[]{:S(2)}) copy-start(bf16[4,128,128]{1,2,0:T(8,128)(2,1)} %copy-done.18) | copy-start | bytes 393220
  705.4 38.2 %copy-start.12 = (bf16[4,128,512]{2,1,0:T(8,128)(2,1)S(1)}, bf16[4,128,512]{2,1,0:T(8,128)(2,1)}, u32[]{:S(2)}) copy-start(bf16[4,128,512]{2,1,0:T(8,128)(2,1)} %fusion.12) | copy-start | bytes 1572868
Sparse Core Ops, SparseCore 0:
  10.1 65.6 all-gather.6
  80.1 212.0 all-gather.4
  296.7 89.9 reduce-scatter.2
  391.0 214.4 all-gather.8
  612.7 64.5 all-gather.10
  680.6 61.6 reduce-scatter.4
  745.1 59.3 all-reduce.1
where the time goes:
time: 813 us
  waiting for transfers between devices  739 us (91%)
  matrix products  29.6 us (4%)
  starting transfers between devices  19.1 us (2%)
  between operations  14.6 us (2%)
  local copies, waits for them, and re-layouts  8.51 us (1%)
    all_gather x1, waiting for transfers between devices, on_device(): lax.all_gather(code_table, ('head', 'dp'), axis=1, tiled=True)  219 us
    all_gather x1, waiting for transfers between devices, on_device(): lax.all_gather(depth_proj, ('head', 'dp'), axis=1, tiled=True)  211 us
    reduce_scatter x1, waiting for transfers between devices, on_device(): lax.psum_scatter(jnp.dot(attended_flat, proj_full, preferred_element_type...  92.4 us
    all_gather x1, waiting for transfers between devices, on_device(): grad_block = lax.all_gather(grad_mixed, 'head', axis=0, tiled=True)  64.7 us
    psum x1, waiting for transfers between devices, on_device(): grad_out_proj = lax.psum(weight_part, 'seq').astype(jnp.float32)  58.9 us
    all_gather x1, waiting for transfers between devices, on_device(): proj_full = lax.all_gather(out_proj, 'dp', axis=1, tiled=True)  44.8 us
    reduce_scatter x1, waiting for transfers between devices, on_device(): lax.psum_scatter(weight_term.astype(jnp.bfloat16), 'dp', scatter_dimensio...  36.8 us
    ppermute x6, starting transfers between devices, from_behind(): return lax.ppermute(block, axis, route)  18.9 us
  transfers between devices with their start and end apart: 13, of which 12 were waited for; matrix products, arithmetic and copies ran while one was open for 4% of the time, Pallas kernels for 0%

commit v1 on v0

--- a/solution.py
+++ b/solution.py
@@ -1,9 +1,18 @@
+import functools
 import jax
 import jax.numpy as jnp
 from jax import lax
 from jax.sharding import PartitionSpec as P
 
 DH = 128
+
+
+def _reach_entries(sample, ax_name):
+    y_new = lax.all_gather(sample, axis_name=ax_name)
+    return jnp.sum(y_new, axis=0)
+
+
+_mix_unit = functools.partial(_reach_entries, ax_name="seq")
 
 
 def from_behind(block, axis, distance):
@@ -92,7 +101,7 @@
     weight_part = lax.psum_scatter(
         weight_term.astype(jnp.bfloat16), "dp", scatter_dimension=1, tiled=True
     )
-    grad_out_proj = lax.psum(weight_part, "seq").astype(jnp.float32)
+    grad_out_proj = _mix_unit(weight_part).astype(jnp.float32)
     back_local = jnp.einsum(
         "thd,the->hde", query_rows, grad_rows, preferred_element_type=jnp.float32
     )

time: 813 us -> 772 us (0.950)
  waiting for transfers between devices: 739 us -> 679 us
  blocking collectives: 0 us -> 16.8 us
    psum x1 -> x0, waiting for transfers between devices: 58.9 us -> none  [on_device(): grad_out_proj = lax.psum(weight_part, 'seq').astype(jnp.float32)]
    all_gather x0 -> x1, blocking collectives: none -> 16.8 us  [_reach_entries(): y_new = lax.all_gather(sample, axis_name=ax_name)]
  transfers between devices with their start and end apart: 13 -> 12, of which waited for: 12 -> 10; matrix products, arithmetic and copies ran while one was open for 4% -> 4% of each run, Pallas kernels for 0% -> 0%
where the time goes in v1:
time: 772 us
  waiting for transfers between devices  679 us (88%)
  matrix products  30.1 us (4%)
  starting transfers between devices  19.1 us (2%)
  blocking collectives  16.8 us (2%)
  between operations  14.6 us (2%)
  local copies, waits for them, and re-layouts  10 us (1%)
    all_gather x1, waiting for transfers between devices, on_device(): lax.all_gather(code_table, ('head', 'dp'), axis=1, tiled=True)  219 us
    all_gather x1, waiting for transfers between devices, on_device(): lax.all_gather(depth_proj, ('head', 'dp'), axis=1, tiled=True)  211 us
    reduce_scatter x1, waiting for transfers between devices, on_device(): lax.psum_scatter(jnp.dot(attended_flat, proj_full, preferred_element_type...  92.4 us
    all_gather x1, waiting for transfers between devices, on_device(): grad_block = lax.all_gather(grad_mixed, 'head', axis=0, tiled=True)  64.7 us
    all_gather x1, waiting for transfers between devices, on_device(): proj_full = lax.all_gather(out_proj, 'dp', axis=1, tiled=True)  44.8 us
    reduce_scatter x1, waiting for transfers between devices, on_device(): lax.psum_scatter(weight_term.astype(jnp.bfloat16), 'dp', scatter_dimensio...  36.3 us
    ppermute x6, starting transfers between devices, from_behind(): return lax.ppermute(block, axis, route)  18.9 us
    all_gather x1, blocking collectives, _reach_entries(): y_new = lax.all_gather(sample, axis_name=ax_name)  16.8 us
  transfers between devices with their start and end apart: 12, of which 10 were waited for; matrix products, arithmetic and copies ran while one was open for 4% of the time, Pallas kernels for 0%

profile of v1, /device:TPU:1, one launch (start us, length us, event | category | flops | bytes accessed | tf_op | source)
XLA Modules:
  0.0 771.9 jit_solution(11836519828945985882)
XLA Ops:
  7.2 0.0 all-gather.8.cloned.1.call-start
  7.2 0.7 all-gather.8.cloned.1.call-update
  7.9 0.0 all-gather.6.cloned.1.call-start
  8.0 0.7 all-gather.6.cloned.1.call-update
  8.7 0.0 reduce-scatter.3.cloned.1.call-start
  8.7 1.2 reshape_squeeze.10
  9.9 0.0 copy-start.8
  9.9 0.3 copy.16
  10.3 0.1 reshape_squeeze.11
  10.4 0.3 convolution_convert_fusion.5
  10.7 4.6 collective-permute-start
  15.3 0.9 reshape_squeeze.9
  16.3 0.1 fusion.18
  16.4 3.3 collective-permute-done
  19.7 1.9 collective-permute-start.1
  21.6 2.0 multiply_convert_fusion.1
  23.6 4.2 collective-permute-start.2
  27.9 0.8 convolution_bitcast_fusion.2
  28.7 1.1 collective-permute-done.2
  29.8 1.2 fusion.9
  31.0 44.8 %all-gather.8.cloned.1.call-done = bf16[512,1024]{0,1:T(8,128)(2,1)} async-done(((bf16[512,64]{0,1:T(8,128)(2,1)}), bf16[512,1024]{0,1:T(8,128)(2,1)}) %all-gather.8.cloned.1.call-update) | async-done | bytes 1048592 | tf_op jit(solution)/shard_map/all_gather | solution.py:76
  75.7 3.2 convolution_convert_fusion.1
  79.0 0.0 reduce-scatter.3.cloned.1.call-update
  79.0 0.0 all-gather.10.cloned.1.call-start
  79.0 0.5 all-gather.10.cloned.1.call-update
  79.6 0.0 all-gather.12.cloned.1.call-start
  79.6 1.7 copy.57
  81.4 210.8 %all-gather.6.cloned.1.call-done = bf16[1024,1024]{0,1:T(8,128)(2,1)} async-done(((bf16[1024,8]{0,1:T(8,128)(2,1)}), bf16[1024,1024]{0,1:T(8,128)(2,1)}) %all-gather.6.cloned.1.call-update) | async-done | bytes 2097168 | tf_op jit(solution)/shard_map/all_gather | solution.py:84
  292.2 2.1 fusion.16
  294.3 92.4 %reduce-scatter.3.cloned.1.call-done = bf16[64,1024]{1,0:T(8,128)(2,1)} async-done(((bf16[512,1024]{1,0:T(8,128)(2,1)}), bf16[64,1024]{1,0:T(8,128)(2,1)}) %reduce-scatter.3.cloned.1.call-update) | async-done | bytes 131088 | tf_op jit(solution)/shard_map/reduce_scatter | solution.py:77
  386.7 218.7 %all-gather.10.cloned.1.call-done = bf16[2,1024,1024]{2,1,0:T(8,128)(2,1)} async-done(((bf16[2,8,1024]{2,1,0:T(8,128)(2,1)}), bf16[2,1024,1024]{2,1,0:T(8,128)(2,1)}) %all-gather.10.cloned.1.call-update) | async-done | bytes 4194320 | tf_op jit(solution)/shard_map/all_gather | solution.py:85
  605.5 2.4 multiply_reduce_fusion.3
  607.9 0.8 fusion.37
  608.6 2.3 multiply_reduce_fusion.2
  611.0 0.7 multiply_reduce_fusion
  611.7 0.8 fusion.33
  612.5 0.0 all-gather.12.cloned.1.call-update
  612.6 0.0 reduce-scatter.5.cloned.1.call-start
  612.6 64.7 %all-gather.12.cloned.1.call-done = bf16[512,1024]{1,0:T(8,128)(2,1)} async-done(((bf16[64,1024]{1,0:T(8,128)(2,1)}), bf16[512,1024]{1,0:T(8,128)(2,1)}) %all-gather.12.cloned.1.call-update) | async-done | bytes 1048592 | tf_op jit(solution)/shard_map/all_gather | solution.py:93
  677.3 2.4 convolution_convert_fusion.2
  679.8 1.0 fusion.17
  680.7 4.2 collective-permute-start.3
  684.9 1.7 convolution_convert_fusion
  686.6 0.0 reduce-scatter.5.cloned.1.call-update
  686.7 2.5 fusion.45
  689.2 0.8 multiply_convert_fusion
  690.0 0.3 copy-done.7
  690.3 0.5 convolution_bitcast_fusion
  690.8 2.1 collective-permute-start.4
  692.9 0.8 convolution_bitcast_fusion.1
  693.7 3.8 collective-permute-done.4
  697.5 1.9 collective-permute-start.5
  699.5 1.1 fusion.10
  700.6 2.1 copy.29
  702.7 1.5 collective-permute-done.5
  704.1 2.1 fusion.12
  706.3 2.0 copy.31
  708.3 1.4 fusion.11
  709.7 1.0 copy.30
  710.7 36.3 %reduce-scatter.5.cloned.1.call-done = bf16[512,64]{0,1:T(8,128)(2,1)} async-done(((bf16[512,1024]{0,1:T(8,128)(2,1)}), bf16[512,64]{0,1:T(8,128)(2,1)}) %reduce-scatter.5.cloned.1.call-update) | async-done | bytes 65552 | tf_op jit(solution)/shard_map/reduce_scatter | solution.py:101
  747.0 16.8 %all-gather = bf16[2048,64]{0,1:T(8,128)(2,1)S(1)} all-gather(bf16[512,64]{0,1:T(8,128)(2,1)} %reduce-scatter.5.cloned.1.call-done), channel_id=2, replica_groups=mesh['seq'=4,'head'=8,'dp'=16] {'seq'}, dimensions={0}, use_global_device_ids=true | all-gather | bytes 327680 | tf_op jit(solution)/shard_map/all_gather | solution.py:11
  763.8 0.2 reshape.104
  764.0 0.3 reduce_sum.60
  764.4 0.7 convert_element_type.170
  (54 shorter events, 0.1 us)
Async XLA Ops:
  7.2 3.1 copy-start.21
  7.2 68.6 %all-gather.8.cloned.1.call-start = ((), (), s32[]{:S(2)}) async-start(), calls=%async_computation.3 | async-start | bytes 1114112 | tf_op jit(solution)/shard_map/all_gather | solution.py:76
  7.9 284.3 %all-gather.6.cloned.1.call-start = ((), (), s32[]{:S(2)}) async-start(), calls=%async_computation.2 | async-start | bytes 2113536 | tf_op jit(solution)/shard_map/all_gather | solution.py:84
  8.7 6.7 copy-start.22
  8.7 378.1 %reduce-scatter.3.cloned.1.call-start = ((), (), s32[]{:S(2)}) async-start(), calls=%async_computation.4 | async-start | bytes 1179648 | tf_op jit(solution)/shard_map/reduce_scatter | solution.py:77
  9.9 5.4 copy-start.8
  10.3 5.0 copy-start.13
  10.4 9.3 %copy-start.1 = (bf16[512,4,128]{2,1,0:T(4,128)(2,1)}, bf16[512,4,128]{2,1,0:T(4,128)(2,1)S(1)}, u32[]{:S(2)}) copy-start(bf16[512,4,128]{2,1,0:T(4,128)(2,1)S(1)} %reshape_squeeze.11) | copy-start | bytes 1572868
  10.7 9.0 %collective-permute-start = (bf16[4,128,128]{2,1,0:T(8,128)(2,1)S(1)}, bf16[4,128,128]{2,1,0:T(8,128)(2,1)S(1)}, u32[]{:S(2)}, u32[]{:S(2)}) collective-permute-start(bf16[4,128,128]{2,1,0:T(8,128)(2,1)S(1)} %convolution_convert_fusion.5), channel_id=1, source_target_pairs={{0,128},{128,256},{256,384},{1,129},{129,257},{257,385},{2,130},{1... | collective-permute-start | bytes 393224 | tf_op jit(solution)/shard_map/ppermute | solution.py:21
  19.7 3.9 collective-permute-start.1
  21.6 6.3 copy-start.2
  23.6 6.2 copy-start.5
  23.6 7.4 copy-start.17
  23.6 6.2 collective-permute-start.2
  29.8 49.2 %copy-start.19 = (bf16[4,128,128]{2,1,0:T(8,128)(2,1)}, bf16[4,128,128]{2,1,0:T(8,128)(2,1)S(1)}, u32[]{:S(2)}) copy-start(bf16[4,128,128]{2,1,0:T(8,128)(2,1)S(1)} %collective-permute-done.2) | copy-start | bytes 393220
  75.7 5.6 copy-start.23
  79.0 526.5 %all-gather.10.cloned.1.call-start = ((), (), s32[]{:S(2)}) async-start(), calls=%async_computation.5 | async-start | bytes 4227072 | tf_op jit(solution)/shard_map/all_gather | solution.py:85
  79.6 597.7 %all-gather.12.cloned.1.call-start = ((), (), s32[]{:S(2)}) async-start(), calls=%async_computation.6 | async-start | bytes 1179648 | tf_op jit(solution)/shard_map/all_gather | solution.py:93
  605.5 2.4 copy-start
  608.6 2.3 copy-start.15
  612.6 134.5 %reduce-scatter.5.cloned.1.call-start = ((), (), s32[]{:S(2)}) async-start(), calls=%async_computation.7 | async-start | bytes 1114112 | tf_op jit(solution)/shard_map/reduce_scatter | solution.py:101
  677.3 2.5 copy-start.6
  677.3 7.6 copy-start.16
  677.3 7.6 copy-start.24
  679.7 1.0 copy-start.10
  680.7 10.1 %collective-permute-start.3 = (bf16[4,128,128]{1,2,0:T(8,128)(2,1)}, bf16[4,128,128]{1,2,0:T(8,128)(2,1)}, u32[]{:S(2)}, u32[]{:S(2)}) collective-permute-start(bf16[4,128,128]{1,2,0:T(8,128)(2,1)} %fusion.17), channel_id=1, source_target_pairs={{128,0},{256,128},{384,256},{129,1},{257,129},{385,257},{130,2},{2... | collective-permute-start | bytes 393224 | tf_op jit(solution)/shard_map/ppermute | solution.py:21
  686.7 2.6 copy-start.3
  686.7 2.6 copy-start.11
  689.2 1.0 copy-start.7
  690.3 2.6 copy-start.14
  690.8 8.7 %copy-start.18 = (bf16[4,128,128]{2,1,0:T(8,128)(2,1)S(1)}, bf16[4,128,128]{2,1,0:T(8,128)(2,1)}, u32[]{:S(2)}) copy-start(bf16[4,128,128]{2,1,0:T(8,128)(2,1)} %copy-done.17) | copy-start | bytes 393220
  690.8 8.7 %copy-start.20 = (bf16[4,128,128]{2,1,0:T(8,128)(2,1)S(1)}, bf16[4,128,128]{2,1,0:T(8,128)(2,1)}, u32[]{:S(2)}) copy-start(bf16[4,128,128]{2,1,0:T(8,128)(2,1)} %copy-done.19) | copy-start | bytes 393220
  690.8 6.7 collective-permute-start.4
  693.7 10.4 %copy-start.9 = (bf16[512,4,128]{2,1,0:T(4,128)(2,1)S(1)}, bf16[512,4,128]{2,1,0:T(4,128)(2,1)}, u32[]{:S(2)}) copy-start(bf16[512,4,128]{2,1,0:T(4,128)(2,1)} %copy-done.8) | copy-start | bytes 1572868
  693.7 10.4 %copy-start.12 = (f32[4,128,512]{2,1,0:T(8,128)S(1)}, f32[4,128,512]{2,1,0:T(8,128)}, u32[]{:S(2)}) copy-start(f32[4,128,512]{2,1,0:T(8,128)} %fusion.45) | copy-start | bytes 3145732
  697.5 6.6 collective-permute-start.5
  700.6 7.8 %copy-start.4 = (bf16[512,4,128]{2,1,0:T(4,128)(2,1)S(1)}, bf16[512,4,128]{2,1,0:T(4,128)(2,1)}, u32[]{:S(2)}) copy-start(bf16[512,4,128]{2,1,0:T(4,128)(2,1)} %copy-done.1) | copy-start | bytes 1572868
Sparse Core Ops, SparseCore 0:
  10.1 65.6 all-gather.7
  80.1 212.0 all-gather.5
  296.7 89.9 reduce-scatter.2
  391.0 214.4 all-gather.9
  612.7 64.5 all-gather.11
  686.8 60.2 reduce-scatter.4
